TPU v7x, 32 devices: a whole 2x2x4 slice. The times are simulated.
32 devices in a mesh: sample: 4 (over x, core), space: 8 (over z, y).
Axes of the slice: x: 2, y: 2, z: 4, core: 2. Of those that a mesh axis runs over, the one named last changes fastest.
Arguments:
- acts: bfloat16 [8, 8, 16, 8, 8, 128], P('sample', 'space'), may hold values from -6 to 6
- weight: float32 [3456, 128], P('space'), may hold values from -0.109375 to 0.109375
- moment: float32 [3456, 128], P('space'), may hold values from -3 to 3
- second: float32 [3456, 128], P('space'), may hold values from 0.05 to 2
- cotangent: bfloat16 [8, 8, 16, 8, 8, 128], P('sample', 'space'), may hold values from -6 to 6
Outputs:
- output: bfloat16 [8, 8, 16, 8, 8, 128], P('sample', 'space')
- input_grad: bfloat16 [8, 8, 16, 8, 8, 128], P('sample', 'space')
- weight_grad: float32 [3456, 128], P('space')
- new_weight: float32 [3456, 128], P('space')
- new_moment: float32 [3456, 128], P('space')
- new_second: float32 [3456, 128], P('space')
All inputs are finite; a program needn't handle non-finite values.
Results may differ from a plain program's by a relative error of at most 0.0062.
Values may be sent and summed in bfloat16 or wider, within the bound.
A program may use at most 64 MiB of HBM per device.

v0:
```python
import functools

import jax
import jax.numpy as jnp
from jax import lax
from jax.experimental import pallas as pl
from jax.experimental.pallas import tpu as pltpu
from jax.sharding import PartitionSpec as P

GY = 2
GZ = 4
MESH = pl.DeviceIdType.MESH
VM = pl.BlockSpec(memory_space=pltpu.VMEM)

root_coef = 0.7978845608
cubic_coef = 0.044715

SIDES = (1, -1)
DIRS = [(0, 1), (0, -1), (1, 0), (-1, 0)] + [(dy, dz) for dy in SIDES for dz in SIDES]


def shifted(value, axis, by):
    devices = lax.axis_size(axis)
    pairs = [(i, i + by) for i in range(devices) if 0 <= i + by < devices]
    return lax.ppermute(value, axis, pairs)


def convolve(field, kernel):
    return lax.conv_general_dilated(
        field,
        kernel,
        (1, 1, 1),
        "VALID",
        dimension_numbers=("NDHWC", "DHWIO", "NDHWC"),
        preferred_element_type=jnp.float32,
    )


def activate(pre):
    inner = root_coef * (pre + cubic_coef * pre * pre * pre)
    tval = jnp.tanh(inner)
    value = 0.5 * pre * (1.0 + tval)
    slope = 0.5 * (1.0 + tval) + 0.5 * pre * (1.0 - tval * tval) * root_coef * (
        1.0 + 3.0 * cubic_coef * pre * pre
    )
    return (value, slope)


def extend_x(field):
    groups = lax.axis_size("space") // (GY * GZ)
    if groups == 1:
        return jnp.pad(field, ((0, 0), (1, 1), (0, 0), (0, 0), (0, 0)))
    coord = lax.axis_index("space") // (GZ * GY)
    length = field.shape[1]
    below = shifted(field[:, length - 1 : length], "space", GY * GZ)
    above = shifted(field[:, :1], "space", -GY * GZ)
    below = jnp.where(coord > 0, below, jnp.zeros_like(below))
    above = jnp.where(coord < groups - 1, above, jnp.zeros_like(above))
    return jnp.concatenate([below, field, above], 1)


def faces(field):
    ends = {1: field.shape[2] - 1, -1: 0}
    endz = {1: field.shape[3] - 1, -1: 0}
    zf = jnp.stack([field[:, :, :, endz[d], :] for d in SIDES])
    yf = jnp.stack([field[:, :, ends[d], :, :] for d in SIDES])
    cf = jnp.stack([field[:, :, ends[dy], endz[dz], :] for dy in SIDES for dz in SIDES])
    return (zf, yf, cf)


def assemble(field, zf, yf, cf):
    mid = jnp.concatenate([zf[0][:, :, :, None], field, zf[1][:, :, :, None]], 3)
    rows = []
    for i in range(2):
        low, high = cf[2 * i][:, :, None, :], cf[2 * i + 1][:, :, None, :]
        rows.append(jnp.concatenate([low, yf[i], high], 2)[:, :, None])
    return jnp.concatenate([rows[0], mid, rows[1]], 2)


class Halo:
    def __init__(self, ins, outs, send, recv):
        me = lax.axis_index("space")
        self.me, self.send, self.recv = me, send, recv
        self.cz, self.cy = lax.rem(me, GZ), lax.rem(me // GZ, GY)
        self.src = [ins[k // 2].at[k % 2] if k < 4 else ins[2].at[k - 4] for k in range(8)]
        self.dst = [outs[k // 2].at[k % 2] if k < 4 else outs[2].at[k - 4] for k in range(8)]

    def has(self, dy, dz):
        y, z = self.cy + dy, self.cz + dz
        return (y >= 0) & (y < GY) & (z >= 0) & (z < GZ)

    def copy(self, k, to):
        return pltpu.make_async_remote_copy(
            src_ref=self.src[k],
            dst_ref=self.dst[k],
            send_sem=self.send.at[k],
            recv_sem=self.recv.at[k],
            device_id={"space": to},
            device_id_type=MESH,
        )

    def start(self):
        for k, (dy, dz) in enumerate(DIRS):

            @pl.when(self.has(dy, dz))
            def _():
                self.copy(k, self.me + dy * GZ + dz).start()

            @pl.when(jnp.logical_not(self.has(-dy, -dz)))
            def _():
                self.dst[k][...] = jnp.zeros(self.dst[k].shape, self.dst[k].dtype)

    def finish(self):
        for k, (dy, dz) in enumerate(DIRS):

            @pl.when(self.has(-dy, -dz))
            def _():
                self.copy(k, self.me).wait_recv()

            @pl.when(self.has(dy, dz))
            def _():
                self.copy(k, self.me).wait_send()


def greet(n, me, sample):
    barrier = pltpu.get_barrier_semaphore()

    def space_peer(d, _):
        pl.semaphore_signal(barrier, 1, device_id={"space": lax.rem(me + d, n)}, device_id_type=MESH)
        return 0

    lax.fori_loop(1, n, space_peer, 0)
    for d in range(1, 4):
        pl.semaphore_signal(barrier, 1, device_id={"sample": lax.rem(sample + d, 4)}, device_id_type=MESH)
    pl.semaphore_wait(barrier, n + 2)


def remote(src, dst, send, recv, **to):
    return pltpu.make_async_remote_copy(
        src_ref=src, dst_ref=dst, send_sem=send, recv_sem=recv, device_id=to, device_id_type=MESH
    )


LAG = 6


def gather_kernel(n, w, zi, yi, ci, out, zo, yo, co, hs, hr, as_, ar, bs, br, cs, cr):
    me, sample = lax.axis_index("space"), lax.axis_index("sample")
    core, x = lax.rem(sample, 2), sample // 2
    across, partner = (1 - x) * 2 + core, x * 2 + 1 - core
    greet(n, me, sample)
    halo = Halo((zi, yi, ci), (zo, yo, co), hs, hr)
    halo.start()

    def first(d, _):
        o = lax.rem(me + d, n)
        remote(w.at[core, x], out.at[me, core, x], as_.at[o], ar.at[me], space=o).start()
        return 0

    lax.fori_loop(1, n, first, 0)
    out[me] = w[...]

    def rest(t, _):
        @pl.when(t < n)
        def _():
            j = lax.rem(me - t + n, n)
            slot = out.at[j, core, x]
            remote(slot, slot, as_.at[j], ar.at[j], space=me).wait_recv()
            remote(slot, slot, bs.at[j], br.at[j], sample=across).start()

        @pl.when(t > LAG)
        def _():
            j = lax.rem(me - t + LAG + n, n)
            slot = out.at[j, core, 1 - x]
            remote(slot, slot, bs.at[j], br.at[j], sample=across).wait_recv()
            pair = out.at[j, core]
            remote(pair, pair, cs.at[j], cr.at[j], sample=partner).start()

        return 0

    lax.fori_loop(1, n + LAG, rest, 0)

    def last(d, _):
        o = lax.rem(me + d, n)
        pair = out.at[o, 1 - core]
        remote(pair, pair, cs.at[o], cr.at[o], sample=partner).wait_recv()
        remote(w.at[core, x], out.at[me, core, x], as_.at[o], ar.at[me], space=o).wait_send()
        slot = out.at[o, core, x]
        remote(slot, slot, bs.at[o], br.at[o], sample=across).wait_send()
        mine = out.at[o, core]
        remote(mine, mine, cs.at[o], cr.at[o], sample=partner).wait_send()
        return 0

    lax.fori_loop(1, n, last, 0)
    halo.finish()


def reduce_kernel(n, g, zi, yi, ci, out, zo, yo, co, r1, s2, r2, s3, r3, hs, hr, as_, ar, bs, br, cs, cr, ds, dr):
    me, sample = lax.axis_index("space"), lax.axis_index("sample")
    core, x = lax.rem(sample, 2), sample // 2
    across, partner = (1 - x) * 2 + core, x * 2 + 1 - core
    f32, bf16 = jnp.float32, jnp.bfloat16
    greet(n, me, sample)
    halo = Halo((zi, yi, ci), (zo, yo, co), hs, hr)
    halo.start()

    def owner(d):
        return lax.rem(me + 1 + d, n)

    def copy1(o):
        return remote(g.at[o, 1 - core], r1.at[o], as_.at[o], ar.at[o], sample=partner)

    def copy2(o):
        return remote(s2.at[o, 1 - x], r2.at[o], bs.at[o], br.at[o], sample=across)

    def copy3(o):
        return remote(s3.at[o], r3.at[me], cs.at[o], cr.at[me], space=o)

    def first(d, _):
        copy1(owner(d)).start()
        return 0

    lax.fori_loop(0, n, first, 0)

    def rest(t, _):
        @pl.when(t < n)
        def _():
            o = owner(t)
            copy1(o).wait_recv()
            s2[o] = (g[o, core].astype(f32) + r1[o].astype(f32)).astype(bf16)
            copy2(o).start()

        @pl.when(t >= LAG)
        def _():
            o = owner(t - LAG)
            copy2(o).wait_recv()
            s3[o] = (s2[o, x].astype(f32) + r2[o].astype(f32)).astype(bf16)

            @pl.when(t < n + LAG - 1)
            def _():
                copy3(o).start()

        return 0

    lax.fori_loop(0, n + LAG, rest, 0)

    def gather(d, total):
        j = lax.rem(me + n - d, n)
        remote(s3.at[j], r3.at[j], cs.at[j], cr.at[j], space=j).wait_recv()
        return total + r3[j].astype(f32)

    out[core, x] = lax.fori_loop(1, n, gather, s3[me].astype(f32))

    def copy4(d):
        mine = out.at[core, x]
        return remote(mine, mine, ds.at[d], dr.at[d], sample=lax.rem(sample + 1 + d, 4))

    for d in range(3):
        copy4(d).start()
    for d in range(3):
        copy4(d).wait()

    def drain(d, _):
        o = owner(d)
        copy1(o).wait_send()
        copy2(o).wait_send()

        @pl.when(d < n - 1)
        def _():
            copy3(o).wait_send()

        return 0

    lax.fori_loop(0, n, drain, 0)
    halo.finish()


def quarters(value, lead):
    rows = value.shape[-2]
    q = -(-rows // 4)
    if rows != 4 * q:
        value = jnp.pad(value, [(0, 0)] * (value.ndim - 2) + [(0, 4 * q - rows), (0, 0)])
    return value.reshape(*lead, 2, 2, q, value.shape[-1])


def whole_rows(value, rows):
    lead = value.shape[:-4]
    return value.reshape(*lead, -1, value.shape[-1])[..., :rows, :]


def like(arrays):
    return [jax.ShapeDtypeStruct(a.shape, a.dtype) for a in arrays]


def sems(*counts):
    return [pltpu.SemaphoreType.DMA((c,)) for c in counts]


def gather_weights(rows_bf, field):
    n = lax.axis_size("space")
    halo = faces(field)
    w = quarters(rows_bf, ())
    whole, zf, yf, cf = pl.pallas_call(
        functools.partial(gather_kernel, n),
        name="gather_and_halo",
        out_shape=[jax.ShapeDtypeStruct((n, *w.shape), w.dtype), *like(halo)],
        in_specs=[VM] * 4,
        out_specs=[VM] * 4,
        scratch_shapes=sems(8, 8, n, n, n, n, n, n),
        compiler_params=pltpu.CompilerParams(collective_id=0, has_side_effects=True),
    )(w, *halo)
    whole = whole_rows(whole, rows_bf.shape[0]).reshape(-1, rows_bf.shape[1])
    return whole, assemble(field, zf, yf, cf)


def reduce_grads(terms, rows, field):
    n = lax.axis_size("space")
    halo = faces(field)
    channels = terms.shape[-1]
    g = quarters(terms.reshape(n, rows, channels), (n,)).astype(jnp.bfloat16)
    q = g.shape[3]
    bf16 = jnp.bfloat16
    total, zf, yf, cf = pl.pallas_call(
        functools.partial(reduce_kernel, n),
        name="reduce_and_halo",
        out_shape=[jax.ShapeDtypeStruct((2, 2, q, channels), jnp.float32), *like(halo)],
        in_specs=[VM] * 4,
        out_specs=[VM] * 4,
        scratch_shapes=[
            pltpu.VMEM((n, 2, q, channels), bf16),
            pltpu.VMEM((n, 2, q, channels), bf16),
            pltpu.VMEM((n, q, channels), bf16),
            pltpu.VMEM((n, q, channels), bf16),
            pltpu.VMEM((n, q, channels), bf16),
            *sems(8, 8, n, n, n, n, n, n, 3, 3),
        ],
        compiler_params=pltpu.CompilerParams(collective_id=1, has_side_effects=True),
    )(g, *halo)
    return whole_rows(total, rows), assemble(field, zf, yf, cf)


def kernel_terms(padded, grad_pre):
    terms = lax.conv_general_dilated(
        padded,
        grad_pre,
        (1, 1, 1),
        "VALID",
        dimension_numbers=("CDHWN", "IDHWO", "DHWNC"),
        preferred_element_type=jnp.float32,
    )
    return terms.reshape(-1, terms.shape[-1])


def local(acts, weight, moment, second, cotangent):
    field = acts[:, 0]
    grad_out = cotangent[:, 0]
    channels = weight.shape[1]
    rows_bf = weight.astype(jnp.bfloat16)
    whole, padded = gather_weights(rows_bf, extend_x(field))
    kernel = whole.reshape(3, 3, 3, channels, channels)
    pre = convolve(padded, kernel)
    value, slope = activate(pre)
    output = value.astype(jnp.bfloat16)
    grad_pre = (grad_out.astype(jnp.float32) * slope).astype(jnp.bfloat16)
    flipped = jnp.flip(kernel, (0, 1, 2)).transpose(0, 1, 2, 4, 3)
    total = (
        field.shape[0]
        * lax.axis_size("sample")
        * lax.axis_size("space")
        * field.shape[1]
        * field.shape[2]
        * field.shape[3]
    )
    local_terms = kernel_terms(padded, grad_pre)
    summed, grad_padded = reduce_grads(local_terms, weight.shape[0], extend_x(grad_pre))
    input_grad = convolve(grad_padded, flipped).astype(jnp.bfloat16)
    weight_grad = summed * float(total) ** (-0.5)
    new_moment = 0.9 * moment + 0.1 * weight_grad
    new_second = 0.999 * second + 0.001 * weight_grad * weight_grad
    first_fix = 1.0 - 0.9**10
    second_fix = 1.0 - 0.999**10
    new_weight = weight - 0.001 * (new_moment / first_fix) / (
        jnp.sqrt(new_second / second_fix) + 1e-08
    )
    return (output[:, None], input_grad[:, None], weight_grad, new_weight, new_moment, new_second)


def solution(mesh):
    in_specs = (
        P("sample", "space", None, None, None, None),
        P("space", None),
        P("space", None),
        P("space", None),
        P("sample", "space", None, None, None, None),
    )
    out_specs = (
        P("sample", "space", None, None, None, None),
        P("sample", "space", None, None, None, None),
        P("space", None),
        P("space", None),
        P("space", None),
        P("space", None),
    )
    return jax.shard_map(local, mesh=mesh, in_specs=in_specs, out_specs=out_specs, check_vma=False)
```

profile of v0, /device:TPU:0, one launch (start us, length us, event | category | flops | bytes accessed | tf_op | source)
XLA Modules:
  0.0 89.5 jit_solution(8828402456523709968)
XLA Ops:
  0.6 1.0 %convert_element_type.26 = bf16[432,128]{1,0:T(8,128)(2,1)S(1)} convert(f32[432,128]{1,0:T(8,128)} %param.6) | non-fusion elementwise | flops 55296 | bytes 331776 | tf_op jit(solution)/shard_map/convert_element_type | solution.py:358
  2.3 1.4 %copy.90 = bf16[2,1,16,8,8,128]{5,2,0,4,3,1:T(8,128)(2,1)S(1)} copy(bf16[2,1,16,8,8,128]{5,4,3,2,1,0:T(8,128)(2,1)} %param.5) | data formatting | bytes 1048576 | tf_op args[0]
  4.4 0.7 copy.42.zi
  5.2 0.7 copy.43.yi
  6.2 22.9 %gather_and_halo.1 = (bf16[8,2,2,108,128]{4,3,2,1,0:T(8,128)(2,1)}, bf16[2,2,18,8,128]{4,3,2,1,0:T(8,128)(2,1)}, bf16[2,2,18,8,128]{4,3,2,1,0:T(8,128)(2,1)}, bf16[4,2,18,128]{3,2,1,0:T(8,128)(2,1)}) custom-call(bf16[2,2,108,128]{3,2,1,0:T(8,128)(2,1)} %reshape.25.w, bf16[2,2,18,8,128]{4,3,2,1,0:T(8,128)(2,1)} %copy.42.zi, ...), custom_call_target="tpu_custom_call" | custom-call | tf_op jit(solution)/shard_map/gather_and_halo/pallas_call | solution.py:303
  29.1 0.8 slice_bitcast_fusion.15
  29.9 0.9 %copy.44 = bf16[2,2,18,8,128]{4,2,1,3,0:T(8,128)(2,1)S(1)} copy(bf16[2,2,18,8,128]{4,3,2,1,0:T(8,128)(2,1)} %get-tuple-element.15) | data formatting | bytes 294912 | tf_op jit(solution)/shard_map/gather_and_halo/pallas_call | solution.py:303
  31.3 0.9 %copy-done.1 = bf16[8,2,2,108,128]{4,3,2,1,0:T(8,128)(2,1)S(1)} copy-done((bf16[8,2,2,108,128]{4,3,2,1,0:T(8,128)(2,1)S(1)}, bf16[8,2,2,108,128]{4,3,2,1,0:T(8,128)(2,1)}, u32[]{:S(2)}) %copy-start.1) | copy-done | bytes 884760
  32.2 1.1 %reshape_reshape_reshape.4 = bf16[3,3,3,128,128]{4,3,2,1,0:T(8,128)(2,1)} reshape(bf16[8,2,2,108,128]{4,3,2,1,0:T(8,128)(2,1)S(1)} %copy-done.1) | data formatting | bytes 1769472 | tf_op jit(solution)/shard_map/reshape;reshape;reshape | solution.py:360
  33.3 7.5 %fusion.12 = f32[2,16,8,8,128]{4,0,3,2,1:T(2,128)S(1)} fusion(bf16[3,3,3,128,128]{4,3,2,1,0:T(8,128)(2,1)} %reshape_reshape_reshape.4, bf16[2,18,10,10,128]{4,1,0,3,2:T(8,128)(2,1)S(1)} %pad_maximum_fusion), kind=kOutput, calls=%fused_computation.20 | convolution fusion | flops 1811939328 | bytes 2854912 | tf_op jit(solution)/shard_map/conv_general_dilated | solution.py:29
  40.8 2.1 %fusion.7 = (bf16[2,16,8,8,128]{4,1,0,3,2:T(8,128)(2,1)S(1)}, bf16[2,1,16,8,8,128]{5,2,0,4,3,1:T(8,128)(2,1)}) fusion(f32[2,16,8,8,128]{4,0,3,2,1:T(2,128)S(1)} %fusion.12, bf16[2,1,16,8,8,128]{5,4,3,2,1,0:T(8,128)(2,1)S(1)} %copy-done.5), kind=kLoop, calls=%fused_computation.13 | loop fusion | flops 5767168 | bytes 2621440 | tf_op jit(solution)/shard_map/convert_element_type | solution.py:364
  42.9 9.0 %convolution_convert_fusion = bf16[3,3,3,128,128]{4,3,2,1,0:T(8,128)(2,1)S(1)} fusion(bf16[2,16,8,8,128]{4,1,0,3,2:T(8,128)(2,1)S(1)} %get-tuple-element.37, bf16[2,18,10,10,128]{4,1,0,3,2:T(8,128)(2,1)S(1)} %pad_maximum_fusion), kind=kOutput, calls=%fused_computation.2 | convolution fusion | flops 1812381696 | bytes 2330624 | tf_op jit(solution)/shard_map/conv_general_dilated | solution.py:343
  51.8 1.0 %copy.67 = bf16[2,1,16,8,8,128]{5,4,3,2,1,0:T(8,128)(2,1)} copy(bf16[2,1,16,8,8,128]{5,2,0,4,3,1:T(8,128)(2,1)S(1)} %copy-done) | data formatting | bytes 1048576
  52.8 1.1 %convert_element_type.32.g = bf16[8,2,2,108,128]{4,3,2,1,0:T(8,128)(2,1)} reshape(bf16[3,3,3,128,128]{4,3,2,1,0:T(8,128)(2,1)S(1)} %convolution_convert_fusion) | data formatting | bytes 1769472 | tf_op jit(solution)/shard_map/convert_element_type | solution.py:320
  54.7 0.7 copy.60.zi
  55.5 0.7 copy.61.yi
  56.2 20.5 %reduce_and_halo.1 = (f32[2,2,108,128]{3,2,1,0:T(8,128)}, bf16[2,2,18,8,128]{4,3,2,1,0:T(8,128)(2,1)}, bf16[2,2,18,8,128]{4,3,2,1,0:T(8,128)(2,1)}, bf16[4,2,18,128]{3,2,1,0:T(8,128)(2,1)}) custom-call(bf16[8,2,2,108,128]{4,3,2,1,0:T(8,128)(2,1)} %convert_element_type.32.g, bf16[2,2,18,8,128]{4,3,2,1,0:T(8,128)(2,1)} %copy.60.zi, ...), custom_call_target="tpu_custom_call" | custom-call | tf_op jit(solution)/shard_map/reduce_and_halo/pallas_call | solution.py:323
  76.7 0.8 slice_bitcast_fusion.11
  77.5 0.9 %copy.62 = bf16[2,2,18,8,128]{4,2,1,3,0:T(8,128)(2,1)S(1)} copy(bf16[2,2,18,8,128]{4,3,2,1,0:T(8,128)(2,1)} %get-tuple-element.19) | data formatting | bytes 294912 | tf_op jit(solution)/shard_map/reduce_and_halo/pallas_call | solution.py:323
  79.2 0.9 %copy-done.2 = bf16[3,3,3,128,128]{4,3,2,1,0:T(8,128)(2,1)S(1)} copy-done((bf16[3,3,3,128,128]{4,3,2,1,0:T(8,128)(2,1)S(1)}, bf16[3,3,3,128,128]{4,3,2,1,0:T(8,128)(2,1)}, u32[]{:S(2)}) %copy-start.2) | copy-done | bytes 884760
  80.1 6.3 %fusion = bf16[2,1,16,8,8,128]{5,0,4,3,2,1:T(2,128)(2,1)S(1)} fusion(bf16[3,3,3,128,128]{4,3,2,1,0:T(8,128)(2,1)S(1)} %copy-done.2, bf16[2,18,10,10,128]{4,1,0,3,2:T(8,128)(2,1)S(1)} %pad_maximum_fusion.1), kind=kOutput, calls=%fused_computation.4 | convolution fusion | flops 1812201472 | bytes 2330624 | tf_op jit(solution)/shard_map/conv_general_dilated | solution.py:29
  86.4 0.9 %copy.68 = bf16[2,1,16,8,8,128]{5,4,3,2,1,0:T(8,128)(2,1)} copy(bf16[2,1,16,8,8,128]{5,0,4,3,2,1:T(2,128)(2,1)S(1)} %fusion) | data formatting | bytes 1048576
  87.5 0.8 copy-done.4
  88.6 0.9 %divide_subtract_fusion = (f32[432,128]{1,0:T(8,128)}, f32[432,128]{1,0:T(8,128)}, f32[432,128]{1,0:T(8,128)}) fusion(f32[432,128]{1,0:T(8,128)S(1)} %copy-done.4, f32[432,128]{1,0:T(8,128)S(1)} %mul.118, f32[432,128]{1,0:T(8,128)S(1)} %copy-done.7, f32[432,128]{1,0:T(8,128)S(1)} %mul.125, f32[432,128]{1,0:T(8,128)S(1)} %mul.113, f32[432,128]{1,0:T(8,128)S(1)} %copy-done.8), kind=kLoop, calls=%fused_computation.38 | loop fusion | flops 552960 | bytes 1990656 | tf_op jit(solution)/shard_map/sub | solution.py:382
  (49 shorter events, 4.1 us)
Async XLA Ops:
  29.1 1.8 %copy-start.9 = (bf16[2,2,18,8,128]{4,3,2,1,0:T(8,128)(2,1)S(1)}, bf16[2,2,18,8,128]{4,3,2,1,0:T(8,128)(2,1)}, u32[]{:S(2)}) copy-start(bf16[2,2,18,8,128]{4,3,2,1,0:T(8,128)(2,1)} %get-tuple-element.16) | copy-start | bytes 442372
  31.0 1.2 %copy-start.1 = (bf16[8,2,2,108,128]{4,3,2,1,0:T(8,128)(2,1)S(1)}, bf16[8,2,2,108,128]{4,3,2,1,0:T(8,128)(2,1)}, u32[]{:S(2)}) copy-start(bf16[8,2,2,108,128]{4,3,2,1,0:T(8,128)(2,1)} %get-tuple-element.17) | copy-start | bytes 2654212
  33.3 7.5 %copy-start.5 = (bf16[2,1,16,8,8,128]{5,4,3,2,1,0:T(8,128)(2,1)S(1)}, bf16[2,1,16,8,8,128]{5,4,3,2,1,0:T(8,128)(2,1)}, u32[]{:S(2)}) copy-start(bf16[2,1,16,8,8,128]{5,4,3,2,1,0:T(8,128)(2,1)} %param.9) | copy-start | bytes 1572868
  42.9 9.0 %copy-start = (bf16[2,1,16,8,8,128]{5,2,0,4,3,1:T(8,128)(2,1)S(1)}, bf16[2,1,16,8,8,128]{5,2,0,4,3,1:T(8,128)(2,1)}, u32[]{:S(2)}) copy-start(bf16[2,1,16,8,8,128]{5,2,0,4,3,1:T(8,128)(2,1)} %get-tuple-element.38) | copy-start | bytes 1572868
  76.7 1.9 %copy-start.10 = (bf16[2,2,18,8,128]{4,3,2,1,0:T(8,128)(2,1)S(1)}, bf16[2,2,18,8,128]{4,3,2,1,0:T(8,128)(2,1)}, u32[]{:S(2)}) copy-start(bf16[2,2,18,8,128]{4,3,2,1,0:T(8,128)(2,1)} %get-tuple-element.20) | copy-start | bytes 442372
  78.9 1.2 %copy-start.2 = (bf16[3,3,3,128,128]{4,3,2,1,0:T(8,128)(2,1)S(1)}, bf16[3,3,3,128,128]{4,3,2,1,0:T(8,128)(2,1)}, u32[]{:S(2)}) copy-start(bf16[3,3,3,128,128]{4,3,2,1,0:T(8,128)(2,1)} %reshape_reshape_reshape.4) | copy-start | bytes 2654212
  80.1 7.3 %copy-start.6 = (f32[2,2,108,128]{3,2,1,0:T(8,128)S(1)}, f32[2,2,108,128]{3,2,1,0:T(8,128)}, u32[]{:S(2)}) copy-start(f32[2,2,108,128]{3,2,1,0:T(8,128)} %get-tuple-element.21) | copy-start | bytes 663556
  87.4 0.9 %copy-start.4 = (f32[432,128]{1,0:T(8,128)S(1)}, f32[432,128]{1,0:T(8,128)}, u32[]{:S(2)}) copy-start(f32[432,128]{1,0:T(8,128)} %param.6) | copy-start | bytes 663556
  87.4 1.1 %copy-start.7 = (f32[432,128]{1,0:T(8,128)S(1)}, f32[432,128]{1,0:T(8,128)}, u32[]{:S(2)}) copy-start(f32[432,128]{1,0:T(8,128)} %param.7) | copy-start | bytes 663556
  87.4 1.2 %copy-start.8 = (f32[432,128]{1,0:T(8,128)S(1)}, f32[432,128]{1,0:T(8,128)}, u32[]{:S(2)}) copy-start(f32[432,128]{1,0:T(8,128)} %param.8) | copy-start | bytes 663556
  87.5 2.0 %copy-start.3 = (f32[432,128]{1,0:T(8,128)}, f32[432,128]{1,0:T(8,128)S(1)}, u32[]{:S(2)}) copy-start(f32[432,128]{1,0:T(8,128)S(1)} %mul.113) | copy-start | bytes 663556
where the time goes:
time: 89.9 us; the launch traced here: 89.5 us
  Pallas kernels  43.4 us (48%)
  matrix products  22.8 us (25%)
  local copies, waits for them, and re-layouts  16.4 us (18%)
  other arithmetic  6 us (7%)
  between operations  0.94 us (1%)
    pallas_call x1, Pallas kernels, gather_weights(): pl.pallas_call(functools.partial(gather_kernel, n), name='gather_and_halo...  22.9 us
    pallas_call x1, Pallas kernels, reduce_grads(): pl.pallas_call(functools.partial(reduce_kernel, n), name='reduce_and_halo...  20.5 us
    conv_general_dilated x2, matrix products, convolve(): lax.conv_general_dilated(field, kernel, (1, 1, 1), 'VALID', dimension_num...  13.8 us
    conv_general_dilated x1, matrix products, kernel_terms(): lax.conv_general_dilated(padded, grad_pre, (1, 1, 1), 'VALID', dimension_...  8.95 us
    unnamed x25, local copies, waits for them, and re-layouts  6.22 us
    convert_element_type x1, other arithmetic, local(): grad_pre = (grad_out.astype(jnp.float32) * slope).astype(jnp.bfloat16)  2.1 us

commit v1 on v0

--- a/solution.py
+++ b/solution.py
@@ -351,7 +351,7 @@
     return terms.reshape(-1, terms.shape[-1])
 
 
-def local(acts, weight, moment, second, cotangent):
+def plain(acts, weight, moment, second, cotangent):
     field = acts[:, 0]
     grad_out = cotangent[:, 0]
     channels = weight.shape[1]
@@ -385,6 +385,556 @@
     return (output[:, None], input_grad[:, None], weight_grad, new_weight, new_moment, new_second)
 
 
+TILE = 16
+
+
+def peers(n):
+    me, sample = lax.axis_index("space"), lax.axis_index("sample")
+    core, x = lax.rem(sample, 2), sample // 2
+    return me, sample, core, x
+
+
+class Field:
+    def __init__(self, block, ends, faces, shifts, send, recv):
+        self.block, self.ends, self.faces, self.shifts = block, ends, faces, shifts
+        self.send, self.recv = send, recv
+        me = lax.axis_index("space")
+        self.me, self.cz, self.cy = me, lax.rem(me, GZ), lax.rem(me // GZ, GY)
+        self.ny = block.shape[2] - 2
+
+    def has(self, dy, dz):
+        y, z = self.cy + dy, self.cz + dz
+        return (y >= 0) & (y < GY) & (z >= 0) & (z < GZ)
+
+    def extract(self):
+        crops, nx, _, nz, _ = self.block.shape
+        row = lax.broadcasted_iota(jnp.int32, (2 * nx, nx * nz), 0)
+        col = lax.broadcasted_iota(jnp.int32, (2 * nx, nx * nz), 1)
+        want = jnp.where(row < nx, row * nz + nz - 1, (row - nx) * nz)
+        pick = jnp.where(col == want, 1.0, 0.0).astype(jnp.bfloat16)
+
+        def step(y, _):
+            for c in range(crops):
+                rows = self.block[c, :, y + 1].reshape(nx * nz, -1)
+                both = jnp.dot(pick, rows, preferred_element_type=jnp.float32).astype(jnp.bfloat16)
+                self.faces[0, y, c] = both[:nx]
+                self.faces[1, y, c] = both[nx:]
+            return 0
+
+        lax.fori_loop(0, self.ny, step, 0)
+
+    def refs(self, dy, dz):
+        last = self.ny - 1
+        if dz == 0:
+            src = self.block.at[:, :, last + 1 if dy > 0 else 1]
+            dst = self.block.at[:, :, 0 if dy > 0 else last + 2]
+            return src, dst
+        side = 0 if dz > 0 else 1
+        if dy == 0:
+            return self.faces.at[side], self.ends.at[side, pl.ds(1, self.ny)]
+        src = self.faces.at[side, last if dy > 0 else 0]
+        return src, self.ends.at[side, 0 if dy > 0 else last + 2]
+
+    def copy(self, k, to):
+        src, dst = self.refs(*DIRS[k])
+        return remote(src, dst, self.send.at[k], self.recv.at[k], space=to)
+
+    def clear(self):
+        for k, (dy, dz) in enumerate(DIRS):
+            dst = self.refs(dy, dz)[1]
+
+            @pl.when(jnp.logical_not(self.has(-dy, -dz)))
+            def _():
+                dst[...] = jnp.zeros(dst.shape, dst.dtype)
+
+        nx = self.block.shape[1]
+        for edge in (0, nx + 1):
+            self.shifts[edge] = jnp.zeros(self.shifts.shape[1:], self.shifts.dtype)
+
+    def start(self, faces_only):
+        for k, (dy, dz) in enumerate(DIRS):
+            if (dz == 0) == faces_only:
+
+                @pl.when(self.has(dy, dz))
+                def _():
+                    self.copy(k, self.me + dy * GZ + dz).start()
+
+    def finish(self):
+        for k, (dy, dz) in enumerate(DIRS):
+
+            @pl.when(self.has(-dy, -dz))
+            def _():
+                self.copy(k, self.me).wait_recv()
+
+    def drain(self):
+        for k, (dy, dz) in enumerate(DIRS):
+
+            @pl.when(self.has(dy, dz))
+            def _():
+                self.copy(k, self.me).wait_send()
+
+    def build(self):
+        crops, nx, _, nz, ch = self.block.shape
+        f32 = jnp.float32
+
+        def step(y, _):
+            out = ([], [], [])
+            for c in range(crops):
+                mid = self.block[c, :, y].astype(f32)
+                low = self.ends[0, y, c].astype(f32)[:, None, :]
+                high = self.ends[1, y, c].astype(f32)[:, None, :]
+                z = lax.broadcasted_iota(jnp.int32, mid.shape, 1)
+                out[0].append(jnp.where(z == 0, low, pltpu.roll(mid, 1, 1)))
+                out[1].append(mid)
+                out[2].append(jnp.where(z == nz - 1, high, pltpu.roll(mid, nz - 1, 1)))
+            for kz in range(3):
+                value = jnp.concatenate(out[kz], 1).astype(jnp.bfloat16)
+                self.shifts[pl.ds(1, nx), y, :, kz * ch : (kz + 1) * ch] = value
+            return 0
+
+        lax.fori_loop(0, self.ny + 2, step, 0)
+
+    def window(self, x0, kx, ky, step):
+        rows = [
+            self.shifts[pl.ds(x0 + kx, step), 2 * p + ky].reshape(-1, self.shifts.shape[-1])
+            for p in range(self.ny // 2)
+        ]
+        return jnp.concatenate(rows, 0)
+
+    def patch(self, x0, step):
+        return jnp.concatenate([self.window(x0, kx, ky, step) for kx in range(3) for ky in range(4)], 1)
+
+
+STEP = 4
+
+
+def fused_kernel(
+    n, scale,
+    acts, cot, w, moment, second,
+    output, igrad, wgrad, nweight, nmoment, nsecond,
+    xb, xe, xf, xs, zb, ze, zf, zs, cotv,
+    wall, w2, w2d, dzt, g, r1, s2, p2, s3, p3, total,
+    ls, xhs, xhr, zhs, zhr,
+    gzs, gzr, gxs, gxr, gys, gyr, gds, gdr, gcs, gcr,
+    c1s, c1r, c2s, c2r, c3s, c3r, c4s, c4r,
+):
+    f32, bf16 = jnp.float32, jnp.bfloat16
+    me, sample, core, x = peers(n)
+    na = n // 2
+    a, b = me // 2, lax.rem(me, 2)
+    across, partner = (1 - x) * 2 + core, x * 2 + 1 - core
+    beside = a * 2 + 1 - b
+    groups = w.shape[0]
+    q = wall.shape[1] // 4
+    ch = w.shape[2]
+    crops, nx, _, nz, _ = xb.shape
+    ny = xb.shape[2] - 2
+
+    load_x = pltpu.make_async_copy(acts, xb.at[:, :, pl.ds(1, ny)], ls.at[0])
+    load_c = pltpu.make_async_copy(cot, cotv, ls.at[1])
+    load_x.start()
+    load_c.start()
+
+    barrier = pltpu.get_barrier_semaphore()
+
+    def greet_space(d, _):
+        pl.semaphore_signal(barrier, 1, device_id={"space": lax.rem(me + d, n)}, device_id_type=MESH)
+        return 0
+
+    lax.fori_loop(1, n, greet_space, 0)
+    for d in range(1, 4):
+        pl.semaphore_signal(barrier, 1, device_id={"sample": lax.rem(sample + d, 4)}, device_id_type=MESH)
+    pl.semaphore_signal(barrier, 1, device_id={"sample": across, "space": beside}, device_id_type=MESH)
+
+    wall[me, pl.ds(0, groups)] = w[...].astype(bf16)
+    wall[me, pl.ds(groups, 4 * q - groups)] = jnp.zeros((4 * q - groups, TILE, ch), bf16)
+    field = Field(xb, xe, xf, xs, xhs, xhr)
+    dfield = Field(zb, ze, zf, zs, zhs, zhr)
+    field.clear()
+    dfield.clear()
+    for kx in range(3):
+        w2[pl.ds((kx * 4 + 3) * 24, 24), :, 0:ch] = jnp.zeros((24, TILE, ch), bf16)
+        w2[pl.ds(kx * 96, 24), :, ch : 2 * ch] = jnp.zeros((24, TILE, ch), bf16)
+        w2d[pl.ds((kx * 4 + 3) * 24, 24), :, 0:ch] = jnp.zeros((24, TILE, ch), bf16)
+        w2d[pl.ds(kx * 96, 24), :, ch : 2 * ch] = jnp.zeros((24, TILE, ch), bf16)
+    g[:, pl.ds(groups, 4 * q - groups)] = jnp.zeros((n, 4 * q - groups, TILE, ch), bf16)
+
+    pl.semaphore_wait(barrier, n + 3)
+
+    def piece(s, c, h):
+        return wall.at[s, pl.ds((c * 2 + h) * q, q)]
+
+    def column(d):
+        return lax.rem(a + na - d, na) * 2 + b
+
+    def other(d):
+        return lax.rem(a + na - d, na) * 2 + 1 - b
+
+    def z_copy(d):
+        part = piece(me, core, x)
+        return remote(part, part, gzs.at[d], gzr.at[d], space=lax.rem(a + d, na) * 2 + b)
+
+    def z_wait(d):
+        part = piece(column(d), core, x)
+        return remote(part, part, gzs.at[d], gzr.at[d], space=beside)
+
+    def x_copy(d):
+        part = piece(column(d), core, x)
+        return remote(part, part, gxs.at[d], gxr.at[d], sample=across)
+
+    def x_wait(d):
+        part = piece(column(d), core, 1 - x)
+        return remote(part, part, gxs.at[d], gxr.at[d], sample=across)
+
+    def y_copy(d):
+        part = piece(column(d), core, x)
+        return remote(part, part, gys.at[d], gyr.at[d], space=beside)
+
+    def y_wait(d):
+        part = piece(other(d), core, x)
+        return remote(part, part, gys.at[d], gyr.at[d], space=beside)
+
+    def d_copy(d):
+        part = piece(column(d), core, x)
+        return remote(part, part, gds.at[d], gdr.at[d], sample=across, space=beside)
+
+    def d_wait(d):
+        part = piece(other(d), core, 1 - x)
+        return remote(part, part, gds.at[d], gdr.at[d], sample=across, space=beside)
+
+    def half(s, c):
+        return wall.at[s, pl.ds(c * 2 * q, 2 * q)]
+
+    def c_copy(i, s):
+        part = half(s, core)
+        return remote(part, part, gcs.at[i], gcr.at[i], sample=partner)
+
+    def c_wait(i, s):
+        part = half(s, 1 - core)
+        return remote(part, part, gcs.at[i], gcr.at[i], sample=partner)
+
+    for d in range(1, na):
+        z_copy(d).start()
+    y_copy(0).start()
+    d_copy(0).start()
+    load_x.wait()
+    field.start(True)
+    field.extract()
+    field.start(False)
+
+    def place(s):
+        def step(i, _):
+            r = s * groups + i
+            at = r + (r // 72) * 24
+            tile = wall[s, i]
+            w2[at, :, 0:ch] = tile
+            w2[at + 24, :, ch : 2 * ch] = tile
+            return 0
+
+        lax.fori_loop(0, groups, step, 0)
+
+    place(me)
+
+    def forward(d, _):
+        z_wait(d).wait_recv()
+        y_copy(d).start()
+        d_copy(d).start()
+        x_copy(d).start()
+        return 0
+
+    lax.fori_loop(1, na, forward, 0)
+    field.finish()
+    field.build()
+
+    def finish_plane(d, _):
+        y_wait(d).wait_recv()
+        d_wait(d).wait_recv()
+        c_copy(na + d, other(d)).start()
+
+        @pl.when(d > 0)
+        def _():
+            x_wait(d).wait_recv()
+            c_copy(d, column(d)).start()
+
+        return 0
+
+    lax.fori_loop(0, na, finish_plane, 0)
+
+    def arrive(d, _):
+        c_wait(na + d, other(d)).wait_recv()
+        place(other(d))
+
+        @pl.when(d > 0)
+        def _():
+            c_wait(d, column(d)).wait_recv()
+            place(column(d))
+
+        return 0
+
+    lax.fori_loop(0, na, arrive, 0)
+
+    load_c.wait()
+    rows = w2.shape[0] * TILE
+
+    def chunk(i, _):
+        x0 = i * STEP
+        pre = jnp.dot(field.patch(x0, STEP), w2[...].reshape(rows, 2 * ch), preferred_element_type=f32)
+        square = pre * pre
+        tval = jnp.tanh(pre * (root_coef + root_coef * cubic_coef * square))
+        gate = 0.5 * (1.0 + tval)
+        value = (pre * gate).astype(bf16)
+        slope = gate + (0.5 * pre) * (1.0 - tval * tval) * (root_coef + 3.0 * root_coef * cubic_coef * square)
+        pieces = []
+        m = STEP * TILE
+        for p in range(ny // 2):
+            line = []
+            for h in range(2):
+                up = jnp.concatenate([cotv[c, pl.ds(x0, STEP), 2 * p + h].astype(f32) for c in range(crops)], 1)
+                dz = up.reshape(m, ch) * slope[p * m : (p + 1) * m, h * ch : (h + 1) * ch]
+                line.append(dz)
+                out = value[p * m : (p + 1) * m, h * ch : (h + 1) * ch].reshape(STEP, TILE, ch)
+                dzr = dz.astype(bf16).reshape(STEP, TILE, ch)
+                for c in range(crops):
+                    output[c, pl.ds(x0, STEP), 2 * p + h] = out[:, c * nz : (c + 1) * nz]
+                    zb[c, pl.ds(x0, STEP), 2 * p + h + 1] = dzr[:, c * nz : (c + 1) * nz]
+            pieces.append(jnp.concatenate(line, 1))
+        dzm = jnp.concatenate(pieces, 0)
+        cols = dzm.shape[0]
+        dzt[:, pl.ds(pl.multiple_of(i * cols, 128), cols)] = dzm.T.astype(bf16)
+        return 0
+
+    lax.fori_loop(0, nx // STEP, chunk, 0)
+
+    dfield.start(True)
+    dfield.extract()
+    dfield.start(False)
+
+    def one(o):
+        return remote(g.at[o, pl.ds((1 - core) * 2 * q, 2 * q)], r1.at[o], c1s.at[o], c1r.at[o], sample=partner)
+
+    def two(k, j):
+        own = j * 2 + (b if k == 0 else 1 - b)
+        side = x if k == 1 else 1 - x
+        to = {"sample": across} if k == 0 else {"space": beside}
+        if k == 2:
+            to = {"sample": across, "space": beside}
+        return remote(s2.at[own, pl.ds(side * q, q)], p2.at[k, j], c2s.at[k, j], c2r.at[k, j], **to)
+
+    def three(d):
+        j = lax.rem(a + d, na)
+        return remote(s3.at[j], p3.at[d], c3s.at[d], c3r.at[d], space=j * 2 + b)
+
+    def four(d):
+        mine = total.at[core * 2 + x]
+        return remote(mine, mine, c4s.at[d], c4r.at[d], sample=lax.rem(sample + 1 + d, 4))
+
+    def send_one(o, _):
+        one(o).start()
+        return 0
+
+    def send_two(o, _):
+        one(o).wait_recv()
+        s2[o] = (g[o, pl.ds(core * 2 * q, 2 * q)].astype(f32) + r1[o].astype(f32)).astype(bf16)
+        j = o // 2
+
+        @pl.when(lax.rem(o, 2) == b)
+        def _():
+            two(0, j).start()
+
+        @pl.when(lax.rem(o, 2) != b)
+        def _():
+            two(2, j).start()
+            two(1, j).start()
+
+        return 0
+
+    def done(kx):
+        return (kx * 72) // groups
+
+    def terms(kx, _):
+        window = [
+            jnp.concatenate([field.window(i * STEP, kx, ky, STEP) for ky in range(4)], 1)
+            for i in range(nx // STEP)
+        ]
+        pair = jnp.dot(dzt[...], jnp.concatenate(window, 0), preferred_element_type=f32)
+        for ky in range(3):
+            k = 3 * ch
+            both = pair[:ch, ky * k : (ky + 1) * k] + pair[ch:, (ky + 1) * k : (ky + 2) * k]
+            for kz in range(3):
+                tap = both[:, kz * ch : (kz + 1) * ch].T.astype(bf16).reshape(ch // TILE, TILE, ch)
+                for t in range(ch // TILE):
+                    r = kx * 72 + (ky * 3 + kz) * (ch // TILE) + t
+                    g[r // groups, lax.rem(r, groups)] = tap[t]
+        lax.fori_loop(done(kx), done(kx + 1), send_one, 0)
+
+        @pl.when(kx > 0)
+        def _():
+            lax.fori_loop(done(kx - 1), done(kx), send_two, 0)
+
+        return 0
+
+    lax.fori_loop(0, 3, terms, 0)
+    lax.fori_loop(done(2), n, send_two, 0)
+
+    def flip(t, _):
+        kx, r = t // 9, lax.rem(t, 9)
+        ky, kz = r // 3, lax.rem(r, 3)
+        src = (kx * 4 + ky) * 24 + kz * 8
+        dst = ((2 - kx) * 4 + 2 - ky) * 24 + (2 - kz) * 8
+        tap = w2[pl.ds(src, 8), :, 0:ch].reshape(ch, ch).astype(f32).T.astype(bf16).reshape(8, TILE, ch)
+        w2d[pl.ds(dst, 8), :, 0:ch] = tap
+        w2d[pl.ds(dst + 24, 8), :, ch : 2 * ch] = tap
+        return 0
+
+    lax.fori_loop(0, 27, flip, 0)
+    dfield.finish()
+    dfield.build()
+
+    def sum_two(j, _):
+        for k in range(3):
+            two(k, j).wait_recv()
+        own = s2[j * 2 + b, pl.ds(x * q, q)].astype(f32)
+        s3[j] = (own + p2[0, j].astype(f32) + p2[1, j].astype(f32) + p2[2, j].astype(f32)).astype(bf16)
+        return 0
+
+    def back(i, _):
+        x0 = i * STEP
+        grad = jnp.dot(
+            dfield.patch(x0, STEP), w2d[...].reshape(rows, 2 * ch), preferred_element_type=f32
+        ).astype(bf16)
+        m = STEP * TILE
+        for p in range(ny // 2):
+            for h in range(2):
+                out = grad[p * m : (p + 1) * m, h * ch : (h + 1) * ch].reshape(STEP, TILE, ch)
+                for c in range(crops):
+                    igrad[c, pl.ds(x0, STEP), 2 * p + h] = out[:, c * nz : (c + 1) * nz]
+
+        @pl.when(i == SUM_AT)
+        def _():
+            lax.fori_loop(0, na, sum_two, 0)
+            for d in range(1, na):
+                three(d).start()
+
+        return 0
+
+    lax.fori_loop(0, nx // STEP, back, 0)
+
+    result = s3[a].astype(f32)
+    for d in range(1, na):
+        three(d).wait_recv()
+        result = result + p3[d].astype(f32)
+    total[core * 2 + x] = result
+    for d in range(3):
+        four(d).start()
+    for d in range(3):
+        four(d).wait()
+    grad = total[...].reshape(4 * q, TILE, ch)[:groups] * scale
+    mom = 0.9 * moment[...] + 0.1 * grad
+    sec = 0.999 * second[...] + 0.001 * grad * grad
+    first_fix = 1.0 - 0.9**10
+    second_fix = 1.0 - 0.999**10
+    wgrad[...] = grad
+    nmoment[...] = mom
+    nsecond[...] = sec
+    nweight[...] = w[...] - 0.001 * (mom / first_fix) / (jnp.sqrt(sec / second_fix) + 1e-08)
+
+    field.drain()
+    dfield.drain()
+    y_copy(0).wait_send()
+    d_copy(0).wait_send()
+
+    def drain_gather(d, _):
+        z_copy(d).wait_send()
+        y_copy(d).wait_send()
+        d_copy(d).wait_send()
+        x_copy(d).wait_send()
+        c_copy(d, column(d)).wait_send()
+        three(d).wait_send()
+        return 0
+
+    lax.fori_loop(1, na, drain_gather, 0)
+
+    def drain_plane(d, _):
+        c_copy(na + d, other(d)).wait_send()
+        for k in range(3):
+            two(k, d).wait_send()
+        return 0
+
+    lax.fori_loop(0, na, drain_plane, 0)
+
+    def drain_one(o, _):
+        one(o).wait_send()
+        return 0
+
+    lax.fori_loop(0, n, drain_one, 0)
+
+
+SUM_AT = 1
+
+
+def fused(acts, weight, moment, second, cotangent, scale):
+    n = lax.axis_size("space")
+    na = n // 2
+    bf16, f32 = jnp.bfloat16, jnp.float32
+    crops, nx, ny, nz, ch = acts.shape
+    groups = weight.shape[0] // TILE
+    q = -(-groups // 4)
+    tiles = [v.reshape(groups, TILE, ch) for v in (weight, moment, second)]
+    state = jax.ShapeDtypeStruct((groups, TILE, ch), f32)
+    block = pltpu.VMEM((crops, nx, ny + 2, nz, ch), bf16)
+    ends = pltpu.VMEM((2, ny + 2, crops, nx, ch), bf16)
+    face = pltpu.VMEM((2, ny, crops, nx, ch), bf16)
+    shifts = pltpu.VMEM((nx + 2, ny + 2, crops * nz, 3 * ch), bf16)
+    wide = pltpu.VMEM((3 * 4 * 3 * ch // TILE, TILE, 2 * ch), bf16)
+    HBM = pl.BlockSpec(memory_space=pl.ANY)
+
+    def sem(*shape):
+        return pltpu.SemaphoreType.DMA(shape)
+
+    outs = pl.pallas_call(
+        functools.partial(fused_kernel, n, scale),
+        name="whole_step",
+        out_shape=[jax.ShapeDtypeStruct(acts.shape, bf16), jax.ShapeDtypeStruct(acts.shape, bf16)] + [state] * 4,
+        in_specs=[HBM, HBM, VM, VM, VM],
+        out_specs=[VM] * 6,
+        scratch_shapes=[
+            block, ends, face, shifts, block, ends, face, shifts,
+            pltpu.VMEM((crops, nx, ny, nz, ch), bf16),
+            pltpu.VMEM((n, 4 * q, TILE, ch), bf16),
+            wide, wide,
+            pltpu.VMEM((2 * ch, crops * nx * ny * nz // 2), bf16),
+            pltpu.VMEM((n, 4 * q, TILE, ch), bf16),
+            pltpu.VMEM((n, 2 * q, TILE, ch), bf16),
+            pltpu.VMEM((n, 2 * q, TILE, ch), bf16),
+            pltpu.VMEM((3, na, q, TILE, ch), bf16),
+            pltpu.VMEM((na, q, TILE, ch), bf16),
+            pltpu.VMEM((na, q, TILE, ch), bf16),
+            pltpu.VMEM((4, q, TILE, ch), f32),
+            sem(2), sem(8), sem(8), sem(8), sem(8),
+            sem(na), sem(na), sem(na), sem(na), sem(na), sem(na), sem(na), sem(na), sem(n), sem(n),
+            sem(n), sem(n), sem(3, na), sem(3, na), sem(na), sem(na), sem(3), sem(3),
+        ],
+        compiler_params=pltpu.CompilerParams(
+            collective_id=2, has_side_effects=True, vmem_limit_bytes=60 * 1024 * 1024
+        ),
+    )(acts, cotangent, *tiles)
+    return list(outs[:2]) + [v.reshape(weight.shape) for v in outs[2:]]
+
+
+def local(acts, weight, moment, second, cotangent):
+    n = lax.axis_size("space")
+    crops, _, nx, ny, nz, channels = acts.shape
+    total = crops * lax.axis_size("sample") * n * nx * ny * nz
+    alone = n == GY * GZ and lax.axis_size("sample") == 4
+    fits = crops * nz == TILE and nx == TILE and ny % 2 == 0 and channels == 128 and weight.shape[0] % TILE == 0
+    if not (alone and fits):
+        return plain(acts, weight, moment, second, cotangent)
+    value, grad, *rest = fused(
+        acts[:, 0], weight, moment, second, cotangent[:, 0], float(total) ** (-0.5)
+    )
+    return (value[:, None], grad[:, None], *rest)
+
+
 def solution(mesh):
     in_specs = (
         P("sample", "space", None, None, None, None),

time: 89.9 us -> 54.1 us (0.60)
  matrix products: 22.8 us -> 0 us
  local copies, waits for them, and re-layouts: 16.4 us -> 6.79 us
  other arithmetic: 6 us -> 0 us
  Pallas kernels: 43.4 us -> 46.4 us
    conv_general_dilated x3 -> x0, matrix products: 22.8 us -> none  [the longest x2 13.8 us: convolve(): lax.conv_general_dilated(field, kernel, (1, 1, 1), 'VALID', dimension_num...]
    another operation x15 -> x0, local copies, waits for them, and re-layouts: 5.77 us -> none  [the longest x2 1.6 us: assemble(): low, high = (cf[2 * i][:, :, None, :], cf[2 * i + 1][:, :, None, :])]
    convert_element_type x2 -> x0, other arithmetic: 3.05 us -> none  [the longest x1 2.1 us: local(): grad_pre = (grad_out.astype(jnp.float32) * slope).astype(jnp.bfloat16)]
    pallas_call x2 -> x1, Pallas kernels: 43.4 us -> 46.4 us  [fused(): pl.pallas_call(functools.partial(fused_kernel, n, scale), name='whole_ste...]
    pallas_call x4 -> x0, local copies, waits for them, and re-layouts: 1.95 us -> none  [the longest x2 0.97 us: reduce_grads(): pl.pallas_call(functools.partial(reduce_kernel, n), name='reduce_and_halo...]
    another operation x6 -> x0, other arithmetic: 1.38 us -> none  [the longest x2 1.27 us: faces(): jnp.stack([field[:, :, ends[dy], endz[dz], :] for dy in SIDES for dz in S...]
    convert_element_type x1 -> x0, local copies, waits for them, and re-layouts: 1.11 us -> none  [reduce_grads(): g = quarters(terms.reshape(n, rows, channels), (n,)).astype(jnp.bfloat16)]
    sub x1 -> x0, other arithmetic: 0.92 us -> none  [local(): weight - 0.001 * (new_moment / first_fix) / (jnp.sqrt(new_second / second...]
where the time goes in v1:
time: 54.1 us; the launch traced here: 53.9 us
  Pallas kernels  46.4 us (86%)
  local copies, waits for them, and re-layouts  6.79 us (13%)
  between operations  0.66 us (1%)
    pallas_call x1, Pallas kernels, fused(): pl.pallas_call(functools.partial(fused_kernel, n, scale), name='whole_ste...  46.4 us
    unnamed x16, local copies, waits for them, and re-layouts  6.79 us

profile of v1, /device:TPU:0, one launch (start us, length us, event | category | flops | bytes accessed | tf_op | source)
XLA Modules:
  0.0 53.9 jit_solution(9414083379390461470)
XLA Ops:
  0.6 46.4 %whole_step.1 = (bf16[2,16,8,8,128]{4,3,2,1,0:T(8,128)(2,1)}, bf16[2,16,8,8,128]{4,3,2,1,0:T(8,128)(2,1)}, f32[27,16,128]{2,1,0:T(8,128)}, f32[27,16,128]{2,1,0:...) custom-call(bf16[2,16,8,8,128]{4,3,2,1,0:T(8,128)(2,1)} %bitcast.15, bf16[2,16,8,8,128]{4,3,2,1,0:T(8,128)(2,1)} %bitcast.16, ...), custom_call_target="tpu_custom_call" | custom-call | tf_op jit(solution)/shard_map/whole_step/pallas_call | solution.py:894
  47.1 0.0 copy-start
  47.1 1.9 %copy.19 = bf16[2,1,16,8,8,128]{5,4,3,2,1,0:T(8,128)(2,1)} copy(bf16[2,1,16,8,8,128]{5,4,3,2,1,0:T(8,128)(2,1)} %bitcast.18) | data formatting | bytes 1048576
  49.0 0.0 copy-done
  49.0 0.0 copy-start.4
  49.0 0.8 %copy.20 = bf16[2,1,16,8,8,128]{5,4,3,2,1,0:T(8,128)(2,1)} copy(bf16[2,1,16,8,8,128]{5,4,3,2,1,0:T(8,128)(2,1)S(1)} %bitcast.17) | data formatting | bytes 1048576
  49.8 0.3 copy-done.4
  50.1 0.0 copy-start.3
  50.1 0.7 %copy.21 = f32[432,128]{1,0:T(8,128)} copy(f32[432,128]{1,0:T(8,128)S(1)} %bitcast.22) | data formatting | bytes 442368
  50.8 0.3 copy-done.3
  51.1 0.0 copy-start.2
  51.1 0.7 %copy.22 = f32[432,128]{1,0:T(8,128)} copy(f32[432,128]{1,0:T(8,128)S(1)} %bitcast.21) | data formatting | bytes 442368
  51.8 0.3 copy-done.2
  52.2 0.0 copy-start.1
  52.2 0.7 %copy.23 = f32[432,128]{1,0:T(8,128)} copy(f32[432,128]{1,0:T(8,128)S(1)} %bitcast.20) | data formatting | bytes 442368
  52.8 0.3 copy-done.1
  53.2 0.7 %copy.24 = f32[432,128]{1,0:T(8,128)} copy(f32[432,128]{1,0:T(8,128)S(1)} %bitcast.19) | data formatting | bytes 442368
Async XLA Ops:
  47.1 1.9 %copy-start = (bf16[2,16,8,8,128]{4,3,2,1,0:T(8,128)(2,1)S(1)}, bf16[2,16,8,8,128]{4,3,2,1,0:T(8,128)(2,1)}, u32[]{:S(2)}) copy-start(bf16[2,16,8,8,128]{4,3,2,1,0:T(8,128)(2,1)} %get-tuple-element.13) | copy-start | bytes 1572868
  49.0 1.1 %copy-start.4 = (f32[27,16,128]{2,1,0:T(8,128)S(1)}, f32[27,16,128]{2,1,0:T(8,128)}, u32[]{:S(2)}) copy-start(f32[27,16,128]{2,1,0:T(8,128)} %get-tuple-element.14) | copy-start | bytes 663556
  50.1 1.0 %copy-start.3 = (f32[27,16,128]{2,1,0:T(8,128)S(1)}, f32[27,16,128]{2,1,0:T(8,128)}, u32[]{:S(2)}) copy-start(f32[27,16,128]{2,1,0:T(8,128)} %get-tuple-element.15) | copy-start | bytes 663556
  51.1 1.0 %copy-start.2 = (f32[27,16,128]{2,1,0:T(8,128)S(1)}, f32[27,16,128]{2,1,0:T(8,128)}, u32[]{:S(2)}) copy-start(f32[27,16,128]{2,1,0:T(8,128)} %get-tuple-element.16) | copy-start | bytes 663556
  52.2 1.0 %copy-start.1 = (f32[27,16,128]{2,1,0:T(8,128)S(1)}, f32[27,16,128]{2,1,0:T(8,128)}, u32[]{:S(2)}) copy-start(f32[27,16,128]{2,1,0:T(8,128)} %get-tuple-element.17) | copy-start | bytes 663556

commit v2 on v1

--- a/solution.py
+++ b/solution.py
@@ -510,9 +510,9 @@
 
 def fused_kernel(
     n, scale,
-    acts, cot, w, moment, second,
+    acts, cot, weight, moment_in, second_in,
     output, igrad, wgrad, nweight, nmoment, nsecond,
-    xb, xe, xf, xs, zb, ze, zf, zs, cotv,
+    xb, xe, xf, xs, zb, ze, zf, zs, cotv, w, moment, second,
     wall, w2, w2d, dzt, g, r1, s2, p2, s3, p3, total,
     ls, xhs, xhr, zhs, zhr,
     gzs, gzr, gxs, gxr, gys, gyr, gds, gdr, gcs, gcr,
@@ -532,8 +532,11 @@
 
     load_x = pltpu.make_async_copy(acts, xb.at[:, :, pl.ds(1, ny)], ls.at[0])
     load_c = pltpu.make_async_copy(cot, cotv, ls.at[1])
-    load_x.start()
-    load_c.start()
+    load_w = pltpu.make_async_copy(weight, w, ls.at[2])
+    load_m = pltpu.make_async_copy(moment_in, moment, ls.at[3])
+    load_s = pltpu.make_async_copy(second_in, second, ls.at[4])
+    for load in (load_w, load_x, load_c, load_m, load_s):
+        load.start()
 
     barrier = pltpu.get_barrier_semaphore()
 
@@ -546,7 +549,6 @@
         pl.semaphore_signal(barrier, 1, device_id={"sample": lax.rem(sample + d, 4)}, device_id_type=MESH)
     pl.semaphore_signal(barrier, 1, device_id={"sample": across, "space": beside}, device_id_type=MESH)
 
-    wall[me, pl.ds(0, groups)] = w[...].astype(bf16)
     wall[me, pl.ds(groups, 4 * q - groups)] = jnp.zeros((4 * q - groups, TILE, ch), bf16)
     field = Field(xb, xe, xf, xs, xhs, xhr)
     dfield = Field(zb, ze, zf, zs, zhs, zhr)
@@ -559,6 +561,8 @@
         w2d[pl.ds(kx * 96, 24), :, ch : 2 * ch] = jnp.zeros((24, TILE, ch), bf16)
     g[:, pl.ds(groups, 4 * q - groups)] = jnp.zeros((n, 4 * q - groups, TILE, ch), bf16)
 
+    load_w.wait()
+    wall[me, pl.ds(0, groups)] = w[...].astype(bf16)
     pl.semaphore_wait(barrier, n + 3)
 
     def piece(s, c, h):
@@ -828,6 +832,8 @@
         four(d).start()
     for d in range(3):
         four(d).wait()
+    load_m.wait()
+    load_s.wait()
     grad = total[...].reshape(4 * q, TILE, ch)[:groups] * scale
     mom = 0.9 * moment[...] + 0.1 * grad
     sec = 0.999 * second[...] + 0.001 * grad * grad
@@ -867,6 +873,15 @@
         return 0
 
     lax.fori_loop(0, n, drain_one, 0)
+
+
+def put_kernel(*refs):
+    k = len(refs) // 2
+    copies = [pltpu.make_async_copy(refs[i], refs[k + i], refs[-1].at[i]) for i in range(k)]
+    for copy in copies:
+        copy.start()
+    for copy in copies:
+        copy.wait()
 
 
 SUM_AT = 1
@@ -886,7 +901,7 @@
     face = pltpu.VMEM((2, ny, crops, nx, ch), bf16)
     shifts = pltpu.VMEM((nx + 2, ny + 2, crops * nz, 3 * ch), bf16)
     wide = pltpu.VMEM((3 * 4 * 3 * ch // TILE, TILE, 2 * ch), bf16)
-    HBM = pl.BlockSpec(memory_space=pl.ANY)
+    HBM = pl.BlockSpec(memory_space=pltpu.HBM)
 
     def sem(*shape):
         return pltpu.SemaphoreType.DMA(shape)
@@ -895,11 +910,12 @@
         functools.partial(fused_kernel, n, scale),
         name="whole_step",
         out_shape=[jax.ShapeDtypeStruct(acts.shape, bf16), jax.ShapeDtypeStruct(acts.shape, bf16)] + [state] * 4,
-        in_specs=[HBM, HBM, VM, VM, VM],
+        in_specs=[HBM] * 5,
         out_specs=[VM] * 6,
         scratch_shapes=[
             block, ends, face, shifts, block, ends, face, shifts,
             pltpu.VMEM((crops, nx, ny, nz, ch), bf16),
+            pltpu.VMEM((groups, TILE, ch), f32), pltpu.VMEM((groups, TILE, ch), f32), pltpu.VMEM((groups, TILE, ch), f32),
             pltpu.VMEM((n, 4 * q, TILE, ch), bf16),
             wide, wide,
             pltpu.VMEM((2 * ch, crops * nx * ny * nz // 2), bf16),
@@ -910,14 +926,23 @@
             pltpu.VMEM((na, q, TILE, ch), bf16),
             pltpu.VMEM((na, q, TILE, ch), bf16),
             pltpu.VMEM((4, q, TILE, ch), f32),
-            sem(2), sem(8), sem(8), sem(8), sem(8),
+            sem(5), sem(8), sem(8), sem(8), sem(8),
             sem(na), sem(na), sem(na), sem(na), sem(na), sem(na), sem(na), sem(na), sem(n), sem(n),
             sem(n), sem(n), sem(3, na), sem(3, na), sem(na), sem(na), sem(3), sem(3),
         ],
         compiler_params=pltpu.CompilerParams(
-            collective_id=2, has_side_effects=True, vmem_limit_bytes=60 * 1024 * 1024
+            collective_id=2, has_side_effects=True, vmem_limit_bytes=32 * 1024 * 1024
         ),
-    )(acts, cotangent, *tiles)
+    )(*[pltpu.with_memory_space_constraint(v, pltpu.HBM) for v in (acts, cotangent, *tiles)])
+    outs = pl.pallas_call(
+        put_kernel,
+        name="put",
+        out_shape=like(outs),
+        in_specs=[VM] * 6,
+        out_specs=[HBM] * 6,
+        scratch_shapes=[sem(6)],
+        compiler_params=pltpu.CompilerParams(vmem_limit_bytes=2 * 1024 * 1024),
+    )(*outs)
     return list(outs[:2]) + [v.reshape(weight.shape) for v in outs[2:]]
 
 

time: 54.1 us -> 46.2 us (0.85)
  local copies, waits for them, and re-layouts: 6.79 us -> 0 us
  Pallas kernels: 46.4 us -> 45.4 us
    unnamed x16 -> x0, local copies, waits for them, and re-layouts: 6.79 us -> none
    pallas_call x1, Pallas kernels: 46.4 us -> 44.1 us  [fused(): pl.pallas_call(functools.partial(fused_kernel, n, scale), name='whole_ste...]
    pallas_call x0 -> x1, Pallas kernels: none -> 1.31 us  [fused(): pl.pallas_call(put_kernel, name='put', out_shape=like(outs), in_specs=[VM...]
where the time goes in v2:
time: 46.2 us; the launch traced here: 46 us
  Pallas kernels  45.4 us (98%)
  between operations  0.64 us (1%)
    pallas_call x1, Pallas kernels, fused(): pl.pallas_call(functools.partial(fused_kernel, n, scale), name='whole_ste...  44.1 us
    pallas_call x1, Pallas kernels, fused(): pl.pallas_call(put_kernel, name='put', out_shape=like(outs), in_specs=[VM...  1.31 us

profile of v2, /device:TPU:0, one launch (start us, length us, event | category | flops | bytes accessed | tf_op | source)
XLA Modules:
  0.0 46.0 jit_solution(1040587510887346468)
XLA Ops:
  0.6 44.1 %whole_step.1 = (bf16[2,16,8,8,128]{4,3,2,1,0:T(8,128)(2,1)S(1)}, bf16[2,16,8,8,128]{4,3,2,1,0:T(8,128)(2,1)S(1)}, f32[27,16,128]{2,1,0:T(8,128)S(1)}, f32[27,16...) custom-call(bf16[2,16,8,8,128]{4,3,2,1,0:T(8,128)(2,1)} %bitcast.15, ...), custom_call_target="tpu_custom_call" | custom-call | tf_op jit(solution)/shard_map/whole_step/pallas_call | solution.py:909
  44.7 1.3 %put.1 = (bf16[2,16,8,8,128]{4,3,2,1,0:T(8,128)(2,1)}, bf16[2,16,8,8,128]{4,3,2,1,0:T(8,128)(2,1)}, f32[27,16,128]{2,1,0:T(8,128)}, f32[27,16,128]{2,1,0:T(8,128...) custom-call(bf16[2,16,8,8,128]{4,3,2,1,0:T(8,128)(2,1)S(1)} %get-tuple-element.18.refs_0_, ...), custom_call_target="tpu_custom_call" | custom-call | tf_op jit(solution)/shard_map/put/pallas_call | solution.py:937

commit v3 on v2

--- a/solution.py
+++ b/solution.py
@@ -413,15 +413,12 @@
         want = jnp.where(row < nx, row * nz + nz - 1, (row - nx) * nz)
         pick = jnp.where(col == want, 1.0, 0.0).astype(jnp.bfloat16)
 
-        def step(y, _):
+        for y in range(self.ny):
             for c in range(crops):
                 rows = self.block[c, :, y + 1].reshape(nx * nz, -1)
                 both = jnp.dot(pick, rows, preferred_element_type=jnp.float32).astype(jnp.bfloat16)
                 self.faces[0, y, c] = both[:nx]
                 self.faces[1, y, c] = both[nx:]
-            return 0
-
-        lax.fori_loop(0, self.ny, step, 0)
 
     def refs(self, dy, dz):
         last = self.ny - 1
@@ -513,7 +510,7 @@
     acts, cot, weight, moment_in, second_in,
     output, igrad, wgrad, nweight, nmoment, nsecond,
     xb, xe, xf, xs, zb, ze, zf, zs, cotv, w, moment, second,
-    wall, w2, w2d, dzt, g, r1, s2, p2, s3, p3, total,
+    wall, w2, wt, dzt, g, r1, s2, p2, s3, p3, total,
     ls, xhs, xhr, zhs, zhr,
     gzs, gzr, gxs, gxr, gys, gyr, gds, gdr, gcs, gcr,
     c1s, c1r, c2s, c2r, c3s, c3r, c4s, c4r,
@@ -552,15 +549,6 @@
     wall[me, pl.ds(groups, 4 * q - groups)] = jnp.zeros((4 * q - groups, TILE, ch), bf16)
     field = Field(xb, xe, xf, xs, xhs, xhr)
     dfield = Field(zb, ze, zf, zs, zhs, zhr)
-    field.clear()
-    dfield.clear()
-    for kx in range(3):
-        w2[pl.ds((kx * 4 + 3) * 24, 24), :, 0:ch] = jnp.zeros((24, TILE, ch), bf16)
-        w2[pl.ds(kx * 96, 24), :, ch : 2 * ch] = jnp.zeros((24, TILE, ch), bf16)
-        w2d[pl.ds((kx * 4 + 3) * 24, 24), :, 0:ch] = jnp.zeros((24, TILE, ch), bf16)
-        w2d[pl.ds(kx * 96, 24), :, ch : 2 * ch] = jnp.zeros((24, TILE, ch), bf16)
-    g[:, pl.ds(groups, 4 * q - groups)] = jnp.zeros((n, 4 * q - groups, TILE, ch), bf16)
-
     load_w.wait()
     wall[me, pl.ds(0, groups)] = w[...].astype(bf16)
     pl.semaphore_wait(barrier, n + 3)
@@ -625,32 +613,45 @@
     field.start(True)
     field.extract()
     field.start(False)
+    field.clear()
+    dfield.clear()
+    for kx in range(3):
+        w2[pl.ds((kx * 4 + 3) * 24, 24), :, 0:ch] = jnp.zeros((24, TILE, ch), bf16)
+        w2[pl.ds(kx * 96, 24), :, ch : 2 * ch] = jnp.zeros((24, TILE, ch), bf16)
+        wt[pl.ds(kx * 12 + 9, 3), pl.ds(0, 8)] = jnp.zeros((3, 8, TILE, ch), bf16)
+        wt[pl.ds(kx * 12, 3), pl.ds(8, 8)] = jnp.zeros((3, 8, TILE, ch), bf16)
+    g[:, pl.ds(groups, 4 * q - groups)] = jnp.zeros((n, 4 * q - groups, TILE, ch), bf16)
+
 
     def place(s):
-        def step(i, _):
+        for i in range(groups):
             r = s * groups + i
             at = r + (r // 72) * 24
             tile = wall[s, i]
             w2[at, :, 0:ch] = tile
             w2[at + 24, :, ch : 2 * ch] = tile
-            return 0
-
-        lax.fori_loop(0, groups, step, 0)
-
-    place(me)
-
-    def forward(d, _):
-        z_wait(d).wait_recv()
-        y_copy(d).start()
-        d_copy(d).start()
-        x_copy(d).start()
-        return 0
-
-    lax.fori_loop(1, na, forward, 0)
-    field.finish()
-    field.build()
-
-    def finish_plane(d, _):
+
+    low_end = 2 * a < na
+
+    def rank(j):
+        return jnp.where(low_end, j, na - 1 - j)
+
+    def forward(j, _):
+        d = lax.rem(a - rank(j) + na, na)
+
+        @pl.when(d > 0)
+        def _():
+            z_wait(d).wait_recv()
+            y_copy(d).start()
+            d_copy(d).start()
+            x_copy(d).start()
+
+        return 0
+
+    lax.fori_loop(0, na, forward, 0)
+
+    def relay(j, _):
+        d = lax.rem(a - rank(j) + na, na)
         y_wait(d).wait_recv()
         d_wait(d).wait_recv()
         c_copy(na + d, other(d)).start()
@@ -662,23 +663,27 @@
 
         return 0
 
-    lax.fori_loop(0, na, finish_plane, 0)
-
-    def arrive(d, _):
+    def arrive(j, _):
+        d = lax.rem(a - rank(j) + na, na)
+
+        @pl.when(d > 0)
+        def _():
+            c_wait(d, column(d)).wait_recv()
+
+        place(column(d))
         c_wait(na + d, other(d)).wait_recv()
         place(other(d))
-
-        @pl.when(d > 0)
-        def _():
-            c_wait(d, column(d)).wait_recv()
-            place(column(d))
-
-        return 0
-
-    lax.fori_loop(0, na, arrive, 0)
-
+        return 0
+
+    lax.fori_loop(0, 2, relay, 0)
+    lax.fori_loop(0, 2, arrive, 0)
+    lax.fori_loop(2, na, relay, 0)
+    field.finish()
+    field.build()
+    lax.fori_loop(2, na, arrive, 0)
     load_c.wait()
     rows = w2.shape[0] * TILE
+    m = STEP * TILE
 
     def chunk(i, _):
         x0 = i * STEP
@@ -689,7 +694,6 @@
         value = (pre * gate).astype(bf16)
         slope = gate + (0.5 * pre) * (1.0 - tval * tval) * (root_coef + 3.0 * root_coef * cubic_coef * square)
         pieces = []
-        m = STEP * TILE
         for p in range(ny // 2):
             line = []
             for h in range(2):
@@ -710,8 +714,6 @@
     lax.fori_loop(0, nx // STEP, chunk, 0)
 
     dfield.start(True)
-    dfield.extract()
-    dfield.start(False)
 
     def one(o):
         return remote(g.at[o, pl.ds((1 - core) * 2 * q, 2 * q)], r1.at[o], c1s.at[o], c1r.at[o], sample=partner)
@@ -771,53 +773,64 @@
                     g[r // groups, lax.rem(r, groups)] = tap[t]
         lax.fori_loop(done(kx), done(kx + 1), send_one, 0)
 
-        @pl.when(kx > 0)
-        def _():
-            lax.fori_loop(done(kx - 1), done(kx), send_two, 0)
+        @pl.when(kx == 0)
+        def _():
+            dfield.extract()
+            dfield.start(False)
+            lax.fori_loop(0, done(1), send_two, 0)
+
+        @pl.when(kx == 2)
+        def _():
+            lax.fori_loop(done(1), done(2), send_two, 0)
 
         return 0
 
     lax.fori_loop(0, 3, terms, 0)
+
+    def flip(t, _):
+        kx = t // 9
+        src = kx * 96 + (t - kx * 9) * 8
+        tap = w2[pl.ds(src, 8), :, 0:ch]
+        back_t = 26 - t
+        col = back_t + (back_t // 9) * 3
+        wt[col, pl.ds(0, 8)] = tap
+        wt[col + 3, pl.ds(8, 8)] = tap
+        return 0
+
+    lax.fori_loop(0, 14, flip, 0)
     lax.fori_loop(done(2), n, send_two, 0)
-
-    def flip(t, _):
-        kx, r = t // 9, lax.rem(t, 9)
-        ky, kz = r // 3, lax.rem(r, 3)
-        src = (kx * 4 + ky) * 24 + kz * 8
-        dst = ((2 - kx) * 4 + 2 - ky) * 24 + (2 - kz) * 8
-        tap = w2[pl.ds(src, 8), :, 0:ch].reshape(ch, ch).astype(f32).T.astype(bf16).reshape(8, TILE, ch)
-        w2d[pl.ds(dst, 8), :, 0:ch] = tap
-        w2d[pl.ds(dst + 24, 8), :, ch : 2 * ch] = tap
-        return 0
-
-    lax.fori_loop(0, 27, flip, 0)
-    dfield.finish()
-    dfield.build()
+    lax.fori_loop(14, 27, flip, 0)
 
     def sum_two(j, _):
         for k in range(3):
             two(k, j).wait_recv()
         own = s2[j * 2 + b, pl.ds(x * q, q)].astype(f32)
         s3[j] = (own + p2[0, j].astype(f32) + p2[1, j].astype(f32) + p2[2, j].astype(f32)).astype(bf16)
-        return 0
+
+        @pl.when(j != a)
+        def _():
+            three(lax.rem(j - a + na, na)).start()
+
+        return 0
+
+    dfield.finish()
+    dfield.build()
 
     def back(i, _):
         x0 = i * STEP
-        grad = jnp.dot(
-            dfield.patch(x0, STEP), w2d[...].reshape(rows, 2 * ch), preferred_element_type=f32
+        taps = jnp.concatenate([wt[k].reshape(2 * ch, ch) for k in range(wt.shape[0])], 1)
+        grad = lax.dot_general(
+            dfield.patch(x0, STEP), taps, (((1,), (1,)), ((), ())), preferred_element_type=f32
         ).astype(bf16)
-        m = STEP * TILE
         for p in range(ny // 2):
             for h in range(2):
                 out = grad[p * m : (p + 1) * m, h * ch : (h + 1) * ch].reshape(STEP, TILE, ch)
                 for c in range(crops):
                     igrad[c, pl.ds(x0, STEP), 2 * p + h] = out[:, c * nz : (c + 1) * nz]
 
-        @pl.when(i == SUM_AT)
-        def _():
-            lax.fori_loop(0, na, sum_two, 0)
-            for d in range(1, na):
-                three(d).start()
+        @pl.when(i >= SUM_AT)
+        def _():
+            lax.fori_loop((i - SUM_AT) * 2, (i - SUM_AT) * 2 + 2, sum_two, 0)
 
         return 0
 
@@ -827,14 +840,14 @@
     for d in range(1, na):
         three(d).wait_recv()
         result = result + p3[d].astype(f32)
-    total[core * 2 + x] = result
+    total[core * 2 + x] = result.astype(bf16)
     for d in range(3):
         four(d).start()
     for d in range(3):
         four(d).wait()
     load_m.wait()
     load_s.wait()
-    grad = total[...].reshape(4 * q, TILE, ch)[:groups] * scale
+    grad = total[...].reshape(4 * q, TILE, ch)[:groups].astype(f32) * scale
     mom = 0.9 * moment[...] + 0.1 * grad
     sec = 0.999 * second[...] + 0.001 * grad * grad
     first_fix = 1.0 - 0.9**10
@@ -875,6 +888,9 @@
     lax.fori_loop(0, n, drain_one, 0)
 
 
+SUM_AT = 2
+
+
 def put_kernel(*refs):
     k = len(refs) // 2
     copies = [pltpu.make_async_copy(refs[i], refs[k + i], refs[-1].at[i]) for i in range(k)]
@@ -882,9 +898,6 @@
         copy.start()
     for copy in copies:
         copy.wait()
-
-
-SUM_AT = 1
 
 
 def fused(acts, weight, moment, second, cotangent, scale):
@@ -917,7 +930,7 @@
             pltpu.VMEM((crops, nx, ny, nz, ch), bf16),
             pltpu.VMEM((groups, TILE, ch), f32), pltpu.VMEM((groups, TILE, ch), f32), pltpu.VMEM((groups, TILE, ch), f32),
             pltpu.VMEM((n, 4 * q, TILE, ch), bf16),
-            wide, wide,
+            wide, pltpu.VMEM((36, 2 * ch // TILE, TILE, ch), bf16),
             pltpu.VMEM((2 * ch, crops * nx * ny * nz // 2), bf16),
             pltpu.VMEM((n, 4 * q, TILE, ch), bf16),
             pltpu.VMEM((n, 2 * q, TILE, ch), bf16),
@@ -925,7 +938,7 @@
             pltpu.VMEM((3, na, q, TILE, ch), bf16),
             pltpu.VMEM((na, q, TILE, ch), bf16),
             pltpu.VMEM((na, q, TILE, ch), bf16),
-            pltpu.VMEM((4, q, TILE, ch), f32),
+            pltpu.VMEM((4, q, TILE, ch), bf16),
             sem(5), sem(8), sem(8), sem(8), sem(8),
             sem(na), sem(na), sem(na), sem(na), sem(na), sem(na), sem(na), sem(na), sem(n), sem(n),
             sem(n), sem(n), sem(3, na), sem(3, na), sem(na), sem(na), sem(3), sem(3),

time: 46.2 us -> 43 us (0.931)
  Pallas kernels: 45.4 us -> 42.2 us
    pallas_call x1, Pallas kernels: 44.1 us -> 40.9 us  [fused(): pl.pallas_call(functools.partial(fused_kernel, n, scale), name='whole_ste...]
where the time goes in v3:
time: 43 us; the launch traced here: 42.8 us
  Pallas kernels  42.2 us (98%)
  between operations  0.64 us (1%)
    pallas_call x1, Pallas kernels, fused(): pl.pallas_call(functools.partial(fused_kernel, n, scale), name='whole_ste...  40.9 us
    pallas_call x1, Pallas kernels, fused(): pl.pallas_call(put_kernel, name='put', out_shape=like(outs), in_specs=[VM...  1.31 us

profile of v3, /device:TPU:0, one launch (start us, length us, event | category | flops | bytes accessed | tf_op | source)
XLA Modules:
  0.0 42.8 jit_solution(13306054044013718724)
XLA Ops:
  0.6 40.9 %whole_step.1 = (bf16[2,16,8,8,128]{4,3,2,1,0:T(8,128)(2,1)S(1)}, bf16[2,16,8,8,128]{4,3,2,1,0:T(8,128)(2,1)S(1)}, f32[27,16,128]{2,1,0:T(8,128)S(1)}, f32[27,16...) custom-call(bf16[2,16,8,8,128]{4,3,2,1,0:T(8,128)(2,1)} %bitcast.15, ...), custom_call_target="tpu_custom_call" | custom-call | tf_op jit(solution)/shard_map/whole_step/pallas_call | solution.py:922
  41.5 1.3 %put.1 = (bf16[2,16,8,8,128]{4,3,2,1,0:T(8,128)(2,1)}, bf16[2,16,8,8,128]{4,3,2,1,0:T(8,128)(2,1)}, f32[27,16,128]{2,1,0:T(8,128)}, f32[27,16,128]{2,1,0:T(8,128...) custom-call(bf16[2,16,8,8,128]{4,3,2,1,0:T(8,128)(2,1)S(1)} %get-tuple-element.18.refs_0_, ...), custom_call_target="tpu_custom_call" | custom-call | tf_op jit(solution)/shard_map/put/pallas_call | solution.py:950

commit v4 on v3

--- a/solution.py
+++ b/solution.py
@@ -502,7 +502,7 @@
         return jnp.concatenate([self.window(x0, kx, ky, step) for kx in range(3) for ky in range(4)], 1)
 
 
-STEP = 4
+STEP = 8
 
 
 def fused_kernel(
@@ -610,7 +610,6 @@
     y_copy(0).start()
     d_copy(0).start()
     load_x.wait()
-    field.start(True)
     field.extract()
     field.start(False)
     field.clear()
@@ -648,7 +647,9 @@
 
         return 0
 
-    lax.fori_loop(0, na, forward, 0)
+    lax.fori_loop(0, 2, forward, 0)
+    field.start(True)
+    lax.fori_loop(2, na, forward, 0)
 
     def relay(j, _):
         d = lax.rem(a - rank(j) + na, na)
@@ -675,12 +676,10 @@
         place(other(d))
         return 0
 
-    lax.fori_loop(0, 2, relay, 0)
-    lax.fori_loop(0, 2, arrive, 0)
-    lax.fori_loop(2, na, relay, 0)
+    lax.fori_loop(0, na, relay, 0)
     field.finish()
     field.build()
-    lax.fori_loop(2, na, arrive, 0)
+    lax.fori_loop(0, na, arrive, 0)
     load_c.wait()
     rows = w2.shape[0] * TILE
     m = STEP * TILE
@@ -708,10 +707,11 @@
             pieces.append(jnp.concatenate(line, 1))
         dzm = jnp.concatenate(pieces, 0)
         cols = dzm.shape[0]
-        dzt[:, pl.ds(pl.multiple_of(i * cols, 128), cols)] = dzm.T.astype(bf16)
-        return 0
-
-    lax.fori_loop(0, nx // STEP, chunk, 0)
+        dzt[:, pl.ds(i * cols, cols)] = dzm.T.astype(bf16)
+        return 0
+
+    for i in range(nx // STEP):
+        chunk(i, 0)
 
     dfield.start(True)
 
@@ -757,7 +757,7 @@
     def done(kx):
         return (kx * 72) // groups
 
-    def terms(kx, _):
+    def terms(kx):
         window = [
             jnp.concatenate([field.window(i * STEP, kx, ky, STEP) for ky in range(4)], 1)
             for i in range(nx // STEP)
@@ -770,22 +770,18 @@
                 tap = both[:, kz * ch : (kz + 1) * ch].T.astype(bf16).reshape(ch // TILE, TILE, ch)
                 for t in range(ch // TILE):
                     r = kx * 72 + (ky * 3 + kz) * (ch // TILE) + t
-                    g[r // groups, lax.rem(r, groups)] = tap[t]
-        lax.fori_loop(done(kx), done(kx + 1), send_one, 0)
-
-        @pl.when(kx == 0)
-        def _():
-            dfield.extract()
-            dfield.start(False)
-            lax.fori_loop(0, done(1), send_two, 0)
-
-        @pl.when(kx == 2)
-        def _():
-            lax.fori_loop(done(1), done(2), send_two, 0)
-
-        return 0
-
-    lax.fori_loop(0, 3, terms, 0)
+                    g[r // groups, r % groups] = tap[t]
+            k = kx * 3 + ky
+            for o in range(k * 24 // groups, (k + 1) * 24 // groups):
+                send_one(o, 0)
+
+    terms(0)
+    dfield.extract()
+    dfield.start(False)
+    lax.fori_loop(0, done(1), send_two, 0)
+    terms(1)
+    terms(2)
+    lax.fori_loop(done(1), done(2), send_two, 0)
 
     def flip(t, _):
         kx = t // 9
@@ -888,7 +884,7 @@
     lax.fori_loop(0, n, drain_one, 0)
 
 
-SUM_AT = 2
+SUM_AT = 0
 
 
 def put_kernel(*refs):

time: 43 us -> 40.4 us (0.940)
  Pallas kernels: 42.2 us -> 39.6 us
    pallas_call x1, Pallas kernels: 40.9 us -> 38.3 us  [fused(): pl.pallas_call(functools.partial(fused_kernel, n, scale), name='whole_ste...]
where the time goes in v4:
time: 40.4 us; the launch traced here: 40.2 us
  Pallas kernels  39.6 us (98%)
  between operations  0.64 us (2%)
    pallas_call x1, Pallas kernels, fused(): pl.pallas_call(functools.partial(fused_kernel, n, scale), name='whole_ste...  38.3 us
    pallas_call x1, Pallas kernels, fused(): pl.pallas_call(put_kernel, name='put', out_shape=like(outs), in_specs=[VM...  1.31 us

profile of v4, /device:TPU:0, one launch (start us, length us, event | category | flops | bytes accessed | tf_op | source)
XLA Modules:
  0.0 40.2 jit_solution(10133018068965629290)
XLA Ops:
  0.6 38.3 %whole_step.1 = (bf16[2,16,8,8,128]{4,3,2,1,0:T(8,128)(2,1)S(1)}, bf16[2,16,8,8,128]{4,3,2,1,0:T(8,128)(2,1)S(1)}, f32[27,16,128]{2,1,0:T(8,128)S(1)}, f32[27,16...) custom-call(bf16[2,16,8,8,128]{4,3,2,1,0:T(8,128)(2,1)} %bitcast.15, ...), custom_call_target="tpu_custom_call" | custom-call | tf_op jit(solution)/shard_map/whole_step/pallas_call | solution.py:918
  38.9 1.3 %put.1 = (bf16[2,16,8,8,128]{4,3,2,1,0:T(8,128)(2,1)}, bf16[2,16,8,8,128]{4,3,2,1,0:T(8,128)(2,1)}, f32[27,16,128]{2,1,0:T(8,128)}, f32[27,16,128]{2,1,0:T(8,128...) custom-call(bf16[2,16,8,8,128]{4,3,2,1,0:T(8,128)(2,1)S(1)} %get-tuple-element.18.refs_0_, ...), custom_call_target="tpu_custom_call" | custom-call | tf_op jit(solution)/shard_map/put/pallas_call | solution.py:946

commit v5 on v4

--- a/solution.py
+++ b/solution.py
@@ -811,6 +811,7 @@
 
     dfield.finish()
     dfield.build()
+    sum_two(0, 0)
 
     def back(i, _):
         x0 = i * STEP
@@ -824,9 +825,7 @@
                 for c in range(crops):
                     igrad[c, pl.ds(x0, STEP), 2 * p + h] = out[:, c * nz : (c + 1) * nz]
 
-        @pl.when(i >= SUM_AT)
-        def _():
-            lax.fori_loop((i - SUM_AT) * 2, (i - SUM_AT) * 2 + 2, sum_two, 0)
+        lax.fori_loop(i + 1, jnp.where(i == 0, 2, na), sum_two, 0)
 
         return 0
 
@@ -882,9 +881,6 @@
         return 0
 
     lax.fori_loop(0, n, drain_one, 0)
-
-
-SUM_AT = 0
 
 
 def put_kernel(*refs):

time: 40.4 us -> 39.5 us (0.978)
  Pallas kernels: 39.6 us -> 38.8 us
    pallas_call x1, Pallas kernels: 38.3 us -> 37.4 us  [fused(): pl.pallas_call(functools.partial(fused_kernel, n, scale), name='whole_ste...]
where the time goes in v5:
time: 39.5 us; the launch traced here: 39.4 us
  Pallas kernels  38.8 us (98%)
  between operations  0.64 us (2%)
    pallas_call x1, Pallas kernels, fused(): pl.pallas_call(functools.partial(fused_kernel, n, scale), name='whole_ste...  37.4 us
    pallas_call x1, Pallas kernels, fused(): pl.pallas_call(put_kernel, name='put', out_shape=like(outs), in_specs=[VM...  1.31 us

profile of v5, /device:TPU:0, one launch (start us, length us, event | category | flops | bytes accessed | tf_op | source)
XLA Modules:
  0.0 39.4 jit_solution(2497832419155214532)
XLA Ops:
  0.6 37.4 %whole_step.1 = (bf16[2,16,8,8,128]{4,3,2,1,0:T(8,128)(2,1)S(1)}, bf16[2,16,8,8,128]{4,3,2,1,0:T(8,128)(2,1)S(1)}, f32[27,16,128]{2,1,0:T(8,128)S(1)}, f32[27,16...) custom-call(bf16[2,16,8,8,128]{4,3,2,1,0:T(8,128)(2,1)} %bitcast.15, ...), custom_call_target="tpu_custom_call" | custom-call | tf_op jit(solution)/shard_map/whole_step/pallas_call | solution.py:914
  38.1 1.3 %put.1 = (bf16[2,16,8,8,128]{4,3,2,1,0:T(8,128)(2,1)}, bf16[2,16,8,8,128]{4,3,2,1,0:T(8,128)(2,1)}, f32[27,16,128]{2,1,0:T(8,128)}, f32[27,16,128]{2,1,0:T(8,128...) custom-call(bf16[2,16,8,8,128]{4,3,2,1,0:T(8,128)(2,1)S(1)} %get-tuple-element.18.refs_0_, ...), custom_call_target="tpu_custom_call" | custom-call | tf_op jit(solution)/shard_map/put/pallas_call | solution.py:942

commit v6 on v5

--- a/solution.py
+++ b/solution.py
@@ -625,7 +625,7 @@
     def place(s):
         for i in range(groups):
             r = s * groups + i
-            at = r + (r // 72) * 24
+            at = r + jnp.where(r >= 144, 48, jnp.where(r >= 72, 24, 0))
             tile = wall[s, i]
             w2[at, :, 0:ch] = tile
             w2[at + 24, :, ch : 2 * ch] = tile
@@ -653,15 +653,15 @@
 
     def relay(j, _):
         d = lax.rem(a - rank(j) + na, na)
+
+        @pl.when(d > 0)
+        def _():
+            x_wait(d).wait_recv()
+            c_copy(d, column(d)).start()
+
         y_wait(d).wait_recv()
         d_wait(d).wait_recv()
         c_copy(na + d, other(d)).start()
-
-        @pl.when(d > 0)
-        def _():
-            x_wait(d).wait_recv()
-            c_copy(d, column(d)).start()
-
         return 0
 
     def arrive(j, _):

time: 39.5 us -> 38.9 us (0.985)
  Pallas kernels: 38.8 us -> 38.1 us
    pallas_call x1, Pallas kernels: 37.4 us -> 36.8 us  [fused(): pl.pallas_call(functools.partial(fused_kernel, n, scale), name='whole_ste...]
where the time goes in v6:
time: 38.9 us; the launch traced here: 38.7 us
  Pallas kernels  38.1 us (98%)
  between operations  0.64 us (2%)
    pallas_call x1, Pallas kernels, fused(): pl.pallas_call(functools.partial(fused_kernel, n, scale), name='whole_ste...  36.8 us
    pallas_call x1, Pallas kernels, fused(): pl.pallas_call(put_kernel, name='put', out_shape=like(outs), in_specs=[VM...  1.31 us

profile of v6, /device:TPU:0, one launch (start us, length us, event | category | flops | bytes accessed | tf_op | source)
XLA Modules:
  0.0 38.7 jit_solution(15290657630343664215)
XLA Ops:
  0.6 36.8 %whole_step.1 = (bf16[2,16,8,8,128]{4,3,2,1,0:T(8,128)(2,1)S(1)}, bf16[2,16,8,8,128]{4,3,2,1,0:T(8,128)(2,1)S(1)}, f32[27,16,128]{2,1,0:T(8,128)S(1)}, f32[27,16...) custom-call(bf16[2,16,8,8,128]{4,3,2,1,0:T(8,128)(2,1)} %bitcast.15, ...), custom_call_target="tpu_custom_call" | custom-call | tf_op jit(solution)/shard_map/whole_step/pallas_call | solution.py:914
  37.4 1.3 %put.1 = (bf16[2,16,8,8,128]{4,3,2,1,0:T(8,128)(2,1)}, bf16[2,16,8,8,128]{4,3,2,1,0:T(8,128)(2,1)}, f32[27,16,128]{2,1,0:T(8,128)}, f32[27,16,128]{2,1,0:T(8,128...) custom-call(bf16[2,16,8,8,128]{4,3,2,1,0:T(8,128)(2,1)S(1)} %get-tuple-element.18.refs_0_, ...), custom_call_target="tpu_custom_call" | custom-call | tf_op jit(solution)/shard_map/put/pallas_call | solution.py:942

commit v7 on v6

--- a/solution.py
+++ b/solution.py
@@ -647,9 +647,10 @@
 
         return 0
 
-    lax.fori_loop(0, 2, forward, 0)
+    place(me)
+    lax.fori_loop(0, 3, forward, 0)
     field.start(True)
-    lax.fori_loop(2, na, forward, 0)
+    lax.fori_loop(3, na, forward, 0)
 
     def relay(j, _):
         d = lax.rem(a - rank(j) + na, na)
@@ -671,7 +672,8 @@
         def _():
             c_wait(d, column(d)).wait_recv()
 
-        place(column(d))
+            place(column(d))
+
         c_wait(na + d, other(d)).wait_recv()
         place(other(d))
         return 0
@@ -825,12 +827,16 @@
                 for c in range(crops):
                     igrad[c, pl.ds(x0, STEP), 2 * p + h] = out[:, c * nz : (c + 1) * nz]
 
-        lax.fori_loop(i + 1, jnp.where(i == 0, 2, na), sum_two, 0)
+        lax.fori_loop(jnp.where(i == 0, 1, 3), jnp.where(i == 0, 3, na), sum_two, 0)
 
         return 0
 
     lax.fori_loop(0, nx // STEP, back, 0)
 
+    load_m.wait()
+    load_s.wait()
+    moment[...] = 0.9 * moment[...]
+    second[...] = 0.999 * second[...]
     result = s3[a].astype(f32)
     for d in range(1, na):
         three(d).wait_recv()
@@ -840,11 +846,9 @@
         four(d).start()
     for d in range(3):
         four(d).wait()
-    load_m.wait()
-    load_s.wait()
     grad = total[...].reshape(4 * q, TILE, ch)[:groups].astype(f32) * scale
-    mom = 0.9 * moment[...] + 0.1 * grad
-    sec = 0.999 * second[...] + 0.001 * grad * grad
+    mom = moment[...] + 0.1 * grad
+    sec = second[...] + 0.001 * grad * grad
     first_fix = 1.0 - 0.9**10
     second_fix = 1.0 - 0.999**10
     wgrad[...] = grad

time: 38.9 us -> 38.8 us (level)
  no operation moved by 1% of the time
where the time goes in v7:
time: 38.8 us; the launch traced here: 38.6 us
  Pallas kernels  38 us (98%)
  between operations  0.64 us (2%)
    pallas_call x1, Pallas kernels, fused(): pl.pallas_call(functools.partial(fused_kernel, n, scale), name='whole_ste...  36.7 us
    pallas_call x1, Pallas kernels, fused(): pl.pallas_call(put_kernel, name='put', out_shape=like(outs), in_specs=[VM...  1.31 us

profile of v7, /device:TPU:0, one launch (start us, length us, event | category | flops | bytes accessed | tf_op | source)
XLA Modules:
  0.0 38.6 jit_solution(14833413322113364647)
XLA Ops:
  0.6 36.7 %whole_step.1 = (bf16[2,16,8,8,128]{4,3,2,1,0:T(8,128)(2,1)S(1)}, bf16[2,16,8,8,128]{4,3,2,1,0:T(8,128)(2,1)S(1)}, f32[27,16,128]{2,1,0:T(8,128)S(1)}, f32[27,16...) custom-call(bf16[2,16,8,8,128]{4,3,2,1,0:T(8,128)(2,1)} %bitcast.15, ...), custom_call_target="tpu_custom_call" | custom-call | tf_op jit(solution)/shard_map/whole_step/pallas_call | solution.py:918
  37.3 1.3 %put.1 = (bf16[2,16,8,8,128]{4,3,2,1,0:T(8,128)(2,1)}, bf16[2,16,8,8,128]{4,3,2,1,0:T(8,128)(2,1)}, f32[27,16,128]{2,1,0:T(8,128)}, f32[27,16,128]{2,1,0:T(8,128...) custom-call(bf16[2,16,8,8,128]{4,3,2,1,0:T(8,128)(2,1)S(1)} %get-tuple-element.18.refs_0_, ...), custom_call_target="tpu_custom_call" | custom-call | tf_op jit(solution)/shard_map/put/pallas_call | solution.py:946
